TPU v7x, 32 devices: a whole 2x2x4 slice. The times are simulated.
32 devices in a mesh: dp: 16 (over z, x, core), tensor: 2 (over y).
Axes of the slice: x: 2, y: 2, z: 4, core: 2. Of those that a mesh axis runs over, the one named last changes fastest.
Arguments:
- tokens: bfloat16 [32768, 1024], P(('dp', 'tensor')), may hold values from -6 to 6
- w_qkv: bfloat16 [1024, 3, 1024], P('dp', None, 'tensor'), may hold values from -0.1875 to 0.1875
- w_out: bfloat16 [1024, 1024], P('tensor', 'dp'), may hold values from -0.75 to 0.75
- w_up: bfloat16 [1024, 4096], P('dp', 'tensor'), may hold values from -0.1875 to 0.1875
- w_down: bfloat16 [4096, 1024], P('tensor', 'dp'), may hold values from -0.09375 to 0.09375
- ln1_gain: float32 [1024], replicated, may hold values from 0.5 to 1.5
- ln1_bias: float32 [1024], replicated, may hold values from -1.5 to 1.5
- ln2_gain: float32 [1024], replicated, may hold values from 0.5 to 1.5
- ln2_bias: float32 [1024], replicated, may hold values from -1.5 to 1.5
- a_qkv: bfloat16 [8, 1024, 16], replicated, may hold values from -0.1875 to 0.1875
- b_qkv: bfloat16 [8, 16, 3, 1024], P(None, None, None, 'tensor'), may hold values from -0.75 to 0.75
- a_out: bfloat16 [8, 1024, 16], P(None, 'tensor'), may hold values from -0.75 to 0.75
- b_out: bfloat16 [8, 16, 1024], replicated, may hold values from -0.75 to 0.75
- a_up: bfloat16 [8, 1024, 16], replicated, may hold values from -0.1875 to 0.1875
- b_up: bfloat16 [8, 16, 4096], P(None, None, 'tensor'), may hold values from -0.75 to 0.75
- a_down: bfloat16 [8, 4096, 16], P(None, 'tensor'), may hold values from -0.09375 to 0.09375
- b_down: bfloat16 [8, 16, 1024], replicated, may hold values from -0.75 to 0.75
- adapter_idx: int32 [16, 4], P('dp'), may hold values from 0 to 7
- pic_start: int32 [16, 2], P('dp'), may hold values from 0 to 1792, as said below
- cotangent: bfloat16 [32768, 1024], P(('dp', 'tensor')), may hold values from -6 to 6
Outputs:
- layer_out: bfloat16 [32768, 1024], P(('dp', 'tensor'))
- grad_tokens: float32 [32768, 1024], P(('dp', 'tensor'))
- grad_a_qkv: float32 [8, 1024, 16], replicated
- grad_b_qkv: float32 [8, 16, 3, 1024], P(None, None, None, 'tensor')
- grad_a_out: float32 [8, 1024, 16], P(None, 'tensor')
- grad_b_out: float32 [8, 16, 1024], replicated
- grad_a_up: float32 [8, 1024, 16], replicated
- grad_b_up: float32 [8, 16, 4096], P(None, None, 'tensor')
- grad_a_down: float32 [8, 4096, 16], P(None, 'tensor')
- grad_b_down: float32 [8, 16, 1024], replicated
Inputs may be any that keep to these rules, and one draw needn't show every extreme that they name: `pic_start`: each sequence has 2 picture spans of 256 tokens; span k starts between k * 1024 and (k + 1) * 1024 - 256, so spans never intersect.
All inputs are finite; a program needn't handle non-finite values.
Results may differ from a plain program's by a relative error of at most 0.014.
Values may be sent and summed in bfloat16 or wider, within the bound.
A program may use at most 320 MiB of HBM per device.

v0:
```python
import jax
import jax.numpy as jnp
from jax import lax
from jax.sharding import PartitionSpec as P

HD = 64
SPAN = 256
BLOCK = 512


def matmul(left, right):
    return jnp.dot(left, right, preferred_element_type=jnp.float32)


def contract_rows(left, right):
    return lax.dot_general(
        left, right, (((0,), (0,)), ((), ())), preferred_element_type=jnp.float32
    )


def against(left, right):
    return lax.dot_general(
        left, right, (((1,), (1,)), ((), ())), preferred_element_type=jnp.float32
    )


def layer_norm(values, multiplier, addend):
    center = values - jnp.mean(values, axis=-1, keepdims=True)
    spread = jnp.mean(center * center, axis=-1, keepdims=True)
    return center * lax.rsqrt(spread + 1e-05) * multiplier + addend


def span_labels(positions, starts):
    inside = (positions[:, None] >= starts[None, :]) & (positions[:, None] < starts[None, :] + SPAN)
    labels = jnp.arange(1, starts.shape[0] + 1, dtype=jnp.int32)
    return jnp.sum(jnp.where(inside, labels[None, :], 0), axis=1)


def allowed_mask(offset, row_count, length, starts):
    row_pos = offset + jnp.arange(row_count, dtype=jnp.int32)
    col_pos = jnp.arange(length, dtype=jnp.int32)
    row_span = span_labels(row_pos, starts)
    col_span = span_labels(col_pos, starts)
    causal = col_pos[None, :] <= row_pos[:, None]
    joined = (row_span[:, None] == col_span[None, :]) & (row_span[:, None] > 0)
    return causal | joined


def masked_scores(query_block, key_rows, offset, length, starts, factor):
    scores = (
        jnp.einsum("qhd,khd->hqk", query_block, key_rows, preferred_element_type=jnp.float32)
        * factor
    )
    allowed = allowed_mask(offset, BLOCK, length, starts)
    return jnp.where(allowed[None], scores, -1000000000.0)


def attend(queries, key_rows, value_rows, starts):
    length, heads, width = queries.shape
    factor = width ** (-0.5)

    def one_block(block_number):
        offset = block_number * BLOCK
        query_block = lax.dynamic_slice_in_dim(queries, offset, BLOCK, 0)
        scores = masked_scores(query_block, key_rows, offset, length, starts, factor)
        peak = jnp.max(scores, axis=-1, keepdims=True)
        raised = jnp.exp(scores - peak)
        totals = jnp.sum(raised, axis=-1, keepdims=True)
        weights_low = (raised / totals).astype(jnp.bfloat16)
        blended = jnp.einsum(
            "hqk,khd->qhd", weights_low, value_rows, preferred_element_type=jnp.float32
        )
        return (
            blended.astype(jnp.bfloat16).reshape(BLOCK, heads * width),
            (peak + jnp.log(totals))[..., 0],
        )

    blended, log_sums = lax.map(one_block, jnp.arange(length // BLOCK, dtype=jnp.int32))
    return (blended.reshape(length, heads * width), log_sums)


def attend_back(queries, key_rows, value_rows, grad_mix, log_sums, starts):
    length, heads, width = queries.shape
    factor = width ** (-0.5)

    def one_block(carry, inputs_pair):
        key_grad, value_grad = carry
        block_number, block_sums = inputs_pair
        offset = block_number * BLOCK
        query_block = lax.dynamic_slice_in_dim(queries, offset, BLOCK, 0)
        grad_block = lax.dynamic_slice_in_dim(grad_mix, offset, BLOCK, 0)
        scores = masked_scores(query_block, key_rows, offset, length, starts, factor)
        weights = jnp.exp(scores - block_sums[:, :, None])
        dots = jnp.einsum(
            "qhd,khd->hqk", grad_block, value_rows, preferred_element_type=jnp.float32
        )
        inner = jnp.sum(weights * dots, axis=-1, keepdims=True)
        slopes = (weights * (dots - inner) * factor).astype(jnp.bfloat16)
        query_grad = jnp.einsum(
            "hqk,khd->qhd", slopes, key_rows, preferred_element_type=jnp.float32
        )
        key_grad = key_grad + jnp.einsum(
            "hqk,qhd->khd", slopes, query_block, preferred_element_type=jnp.float32
        )
        value_grad = value_grad + jnp.einsum(
            "hqk,qhd->khd",
            weights.astype(jnp.bfloat16),
            grad_block,
            preferred_element_type=jnp.float32,
        )
        return ((key_grad, value_grad), query_grad)

    initial = jnp.zeros(key_rows.shape, jnp.float32)
    numbers = jnp.arange(length // BLOCK, dtype=jnp.int32)
    (key_grad, value_grad), query_grad = lax.scan(
        one_block, (initial, initial), (numbers, log_sums)
    )
    return (query_grad.reshape(length, heads, width), key_grad, value_grad)


def fetch_frozen(first, second):
    return (
        lax.all_gather(first, "dp", axis=0, tiled=True),
        lax.all_gather(second, "dp", axis=1, tiled=True),
    )


def enter_rows(normed, reduced):
    return (
        lax.all_gather(normed, "tensor", axis=0, tiled=True),
        lax.all_gather(reduced, "tensor", axis=0, tiled=True),
    )


def leave_rows(partial_value, reduced):
    return (
        lax.psum_scatter(partial_value, "tensor", scatter_dimension=0, tiled=True),
        lax.psum_scatter(reduced, "tensor", scatter_dimension=0, tiled=True),
    )


def enter_grads(branch, reduced):
    return (
        lax.all_gather(branch, "tensor", axis=0, tiled=True),
        lax.all_gather(reduced, "tensor", axis=0, tiled=True),
    )


def leave_grads(partial_value, reduced):
    return (
        lax.psum_scatter(partial_value, "tensor", scatter_dimension=0, tiled=True),
        lax.psum_scatter(reduced, "tensor", scatter_dimension=0, tiled=True),
    )


def per_device(
    tokens,
    w_qkv,
    w_out,
    w_up,
    w_down,
    ln1_gain,
    ln1_bias,
    ln2_gain,
    ln2_bias,
    a_qkv,
    b_qkv,
    a_out,
    b_out,
    a_up,
    b_up,
    a_down,
    b_down,
    adapter_idx,
    pic_start,
    cotangent,
):
    selection = adapter_idx[0]
    starts = pic_start[0]

    def chosen(stacked, which_one):
        return lax.dynamic_index_in_dim(stacked, selection[which_one], 0, keepdims=False)

    low_qkv_in = chosen(a_qkv, 0)
    rank = low_qkv_in.shape[1]
    low_qkv_out = chosen(b_qkv, 0).reshape(rank, -1)
    low_out_in = chosen(a_out, 1)
    low_out_out = chosen(b_out, 1)
    low_up_in = chosen(a_up, 2)
    low_up_out = chosen(b_up, 2)
    low_down_in = chosen(a_down, 3)
    low_down_out = chosen(b_down, 3)
    heads_here = low_out_in.shape[0] // HD

    def run_forward(own_tokens, frozen):
        qkv_rows, out_rows, up_rows, down_rows = frozen
        qkv_full, out_full = fetch_frozen(qkv_rows, out_rows)
        qkv_flat = qkv_full.reshape(qkv_full.shape[0], -1)
        own_float = own_tokens.astype(jnp.float32)
        normed = layer_norm(own_float, ln1_gain, ln1_bias).astype(jnp.bfloat16)
        reduced = matmul(normed, low_qkv_in).astype(jnp.bfloat16)
        normed_all, reduced_all = enter_rows(normed, reduced)
        length = normed_all.shape[0]
        project = (matmul(normed_all, qkv_flat) + matmul(reduced_all, low_qkv_out)).astype(
            jnp.bfloat16
        )
        split = project.reshape(length, 3, heads_here, HD)
        blended, log_sums = attend(split[:, 0], split[:, 1], split[:, 2], starts)
        main_part, low_part = leave_rows(matmul(blended, out_full), matmul(blended, low_out_in))
        low_out_val = low_part.astype(jnp.bfloat16)
        residual = own_float + main_part + matmul(low_out_val, low_out_out)
        up_full, down_full = fetch_frozen(up_rows, down_rows)
        normed_two = layer_norm(residual, ln2_gain, ln2_bias).astype(jnp.bfloat16)
        reduced_two = matmul(normed_two, low_up_in).astype(jnp.bfloat16)
        normed_two_all, reduced_two_all = enter_rows(normed_two, reduced_two)
        pre_act = matmul(normed_two_all, up_full) + matmul(reduced_two_all, low_up_out)
        hidden = jax.nn.gelu(pre_act, approximate=True).astype(jnp.bfloat16)
        main_two, low_two = leave_rows(matmul(hidden, down_full), matmul(hidden, low_down_in))
        low_down_val = low_two.astype(jnp.bfloat16)
        output = residual + main_two + matmul(low_down_val, low_down_out)
        kept_state = (
            qkv_flat,
            out_full,
            up_full,
            down_full,
            normed,
            reduced_all,
            split,
            blended,
            log_sums,
            low_out_val,
            residual,
            normed_two,
            reduced_two_all,
            pre_act,
            hidden,
            low_down_val,
        )
        return (output, kept_state)

    frozen = (w_qkv, w_out, w_up, w_down)
    output, kept_state = run_forward(tokens, frozen)
    fresh_tokens, fresh_frozen = lax.optimization_barrier((tokens, frozen))
    repeat_out, kept_state = run_forward(fresh_tokens, fresh_frozen)
    (
        qkv_flat,
        out_full,
        up_full,
        down_full,
        normed,
        reduced_all,
        split,
        blended,
        log_sums,
        low_out_val,
        residual,
        normed_two,
        reduced_two_all,
        pre_act,
        hidden,
        low_down_val,
    ) = kept_state
    cot_float = cotangent.astype(jnp.float32)
    grad_low_down = against(cotangent, low_down_out).astype(jnp.bfloat16)
    grad_b_down_here = contract_rows(low_down_val, cotangent)
    cot_all, grad_low_down_all = enter_grads(cotangent, grad_low_down)
    grad_hidden = against(cot_all, down_full) + against(grad_low_down_all, low_down_in)
    grad_a_down_here = contract_rows(hidden, grad_low_down_all)
    gelu_pull = jax.vjp(lambda inner_val: jax.nn.gelu(inner_val, approximate=True), pre_act)[1]
    grad_pre = gelu_pull(grad_hidden)[0].astype(jnp.bfloat16)
    grad_b_up_here = contract_rows(reduced_two_all, grad_pre)
    grad_normed_two, grad_reduced_two = leave_grads(
        against(grad_pre, up_full), against(grad_pre, low_up_out)
    )
    grad_low_up = grad_reduced_two.astype(jnp.bfloat16)
    grad_a_up_here = contract_rows(normed_two, grad_low_up)
    grad_normed_two = grad_normed_two + against(grad_low_up, low_up_in)
    norm_pull_two = jax.vjp(lambda inner_val: layer_norm(inner_val, ln2_gain, ln2_bias), residual)[
        1
    ]
    grad_resid = cot_float + norm_pull_two(grad_normed_two)[0]
    branch_low = grad_resid.astype(jnp.bfloat16)
    grad_low_out = against(branch_low, low_out_out).astype(jnp.bfloat16)
    grad_b_out_here = contract_rows(low_out_val, branch_low)
    branch_all, grad_low_out_all = enter_grads(branch_low, grad_low_out)
    grad_mix = (against(branch_all, out_full) + against(grad_low_out_all, low_out_in)).astype(
        jnp.bfloat16
    )
    grad_a_out_here = contract_rows(blended, grad_low_out_all)
    length = grad_mix.shape[0]
    query_grad, key_grad, value_grad = attend_back(
        split[:, 0],
        split[:, 1],
        split[:, 2],
        grad_mix.reshape(length, heads_here, HD),
        log_sums,
        starts,
    )
    grad_qkv = (
        jnp.stack([query_grad, key_grad, value_grad], axis=1)
        .reshape(length, -1)
        .astype(jnp.bfloat16)
    )
    grad_b_qkv_here = contract_rows(reduced_all, grad_qkv)
    grad_normed_one, grad_reduced_one = leave_grads(
        against(grad_qkv, qkv_flat), against(grad_qkv, low_qkv_out)
    )
    grad_low_qkv = grad_reduced_one.astype(jnp.bfloat16)
    grad_a_qkv_here = contract_rows(normed, grad_low_qkv)
    grad_normed_one = grad_normed_one + against(grad_low_qkv, low_qkv_in)
    norm_pull_one = jax.vjp(
        lambda inner_val: layer_norm(inner_val, ln1_gain, ln1_bias), tokens.astype(jnp.float32)
    )[1]
    grad_input = grad_resid + norm_pull_one(grad_normed_one)[0]
    slots = a_qkv.shape[0]

    def spread(gradient, which_one):
        onehot = (jnp.arange(slots, dtype=jnp.int32) == selection[which_one]).astype(jnp.float32)
        return onehot.reshape((slots,) + (1,) * gradient.ndim) * gradient[None]

    sharded = (
        lax.psum(spread(grad_b_qkv_here.reshape(rank, 3, -1), 0).astype(jnp.bfloat16), "dp").astype(
            jnp.float32
        ),
        lax.psum(spread(grad_a_out_here, 1).astype(jnp.bfloat16), "dp").astype(jnp.float32),
        lax.psum(spread(grad_b_up_here, 2).astype(jnp.bfloat16), "dp").astype(jnp.float32),
        lax.psum(spread(grad_a_down_here, 3).astype(jnp.bfloat16), "dp").astype(jnp.float32),
    )
    shared = lax.psum(
        (
            spread(grad_a_qkv_here, 0),
            spread(grad_b_out_here, 1),
            spread(grad_a_up_here, 2),
            spread(grad_b_down_here, 3),
        ),
        ("dp", "tensor"),
    )
    return (
        output.astype(jnp.bfloat16),
        grad_input,
        shared[0],
        sharded[0],
        sharded[1],
        shared[1],
        shared[2],
        sharded[2],
        sharded[3],
        shared[3],
    )


def solution(mesh):
    placed = (
        P(("dp", "tensor"), None),
        P("dp", None, "tensor"),
        P("tensor", "dp"),
        P("dp", "tensor"),
        P("tensor", "dp"),
        P(),
        P(),
        P(),
        P(),
        P(),
        P(None, None, None, "tensor"),
        P(None, "tensor", None),
        P(),
        P(),
        P(None, None, "tensor"),
        P(None, "tensor", None),
        P(),
        P("dp", None),
        P("dp", None),
        P(("dp", "tensor"), None),
    )
    return jax.shard_map(
        per_device,
        mesh=mesh,
        in_specs=placed,
        out_specs=(
            P(("dp", "tensor"), None),
            P(("dp", "tensor"), None),
            P(),
            P(None, None, None, "tensor"),
            P(None, "tensor", None),
            P(),
            P(),
            P(None, None, "tensor"),
            P(None, "tensor", None),
            P(),
        ),
        check_vma=False,
    )
```

profile of v0, /device:TPU:0, one launch (start us, length us, event | category | flops | bytes accessed | tf_op | source)
XLA Modules:
  0.0 2568.8 jit_solution(11967599070437223480)
XLA Ops:
  63.1 52.4 %all-gather.31.cloned.1.call-done = bf16[2048,1024]{1,0:T(8,128)(2,1)} async-done(((bf16[1024,1024]{1,0:T(8,128)(2,1)}), bf16[2048,1024]{1,0:T(8,128)(2,1)}) %all-gather.31.cloned.1.call-update) | async-done | bytes 4194320 | tf_op jit(solution)/shard_map/all_gather | solution.py:130
  131.2 196.5 %while.38 = (s32[]{:T(128)}, bf16[4,512,512]{2,1,0:T(8,128)(2,1)}, f32[4,8,512]{2,1,0:T(8,128)S(1)}, s32[4]{0:T(128)S(1)}, s32[1,2]{1,0:T(1,128)S(1)}, /*index=5...) while((s32[]{:T(128)}, bf16[4,512,512]{2,1,0:T(8,128)(2,1)}, ...), condition=%wide.region_21.22_spmd, body=%wide.region_16.21_spmd.sunk | while | flops 2252623360 | bytes 112358664 | solution.py:78
  341.2 101.4 %reduce-scatter.20.cloned.1.call-done = f32[1024,1024]{1,0:T(8,128)} async-done(((f32[2048,1024]{1,0:T(8,128)}), f32[1024,1024]{1,0:T(8,128)}) %reduce-scatter.20.cloned.1.call-update) | async-done | bytes 4194320 | tf_op jit(solution)/shard_map/reduce_scatter | solution.py:137
  495.5 56.9 %all-gather.37.cloned.1.call-done = bf16[2048,1024]{1,0:T(8,128)(2,1)} async-done(((bf16[1024,1024]{1,0:T(8,128)(2,1)}), bf16[2048,1024]{1,0:T(8,128)(2,1)}) %all-gather.37.cloned.1.call-update) | async-done | bytes 4194320 | tf_op jit(solution)/shard_map/all_gather | solution.py:130
  610.8 53.0 %all-gather.27.cloned.1.call-done = bf16[2048,1024]{0,1:T(8,128)(2,1)} async-done(((bf16[2048,64]{0,1:T(8,128)(2,1)}), bf16[2048,1024]{0,1:T(8,128)(2,1)}) %all-gather.27.cloned.1.call-update) | async-done | bytes 4194320 | tf_op jit(solution)/shard_map/all_gather | solution.py:124
  709.1 97.8 %reduce-scatter.24.cloned.1.call-done = f32[1024,1024]{1,0:T(8,128)} async-done(((f32[2048,1024]{1,0:T(8,128)}), f32[1024,1024]{1,0:T(8,128)}) %reduce-scatter.24.cloned.1.call-update) | async-done | bytes 4194320 | tf_op jit(solution)/shard_map/reduce_scatter | solution.py:151
  824.3 49.9 %all-gather.41.cloned.1.call-done = bf16[2048,1024]{1,0:T(8,128)(2,1)} async-done(((bf16[1024,1024]{1,0:T(8,128)(2,1)}), bf16[2048,1024]{1,0:T(8,128)(2,1)}) %all-gather.41.cloned.1.call-update) | async-done | bytes 4194320 | tf_op jit(solution)/shard_map/all_gather | solution.py:144
  881.9 636.9 %while.39 = (s32[]{:T(128)}, f32[2048,8,64]{0,2,1:T(8,128)}, f32[2048,8,64]{0,2,1:T(8,128)}, bf16[4,512,8,64]{1,0,3,2:T(4,128)(2,1)}, s32[4]{0:T(128)S(1)}, /*in...) while((s32[]{:T(128)}, f32[2048,8,64]{0,2,1:T(8,128)}, ...), condition=%wide.region_34.35_spmd.clone, body=%wide.region_30.34_spmd.clone.sunk | while | flops 5494574592 | bytes 331953440 | solution.py:115
  932.2 42.6 %fusion.336 = bf16[1,512,8,64]{1,3,2,0:T(8,128)(2,1)S(1)} fusion(bf16[2048,8,64]{0,2,1:T(8,128)(2,1)} %get-tuple-element.550, f32[8,512,2048]{2,1,0:T(8,128)} %subtract_exponential_fusion.4, f32[8,512,2048]{2,1,0:T(8,128)} %fusion.335), kind=kOutput, calls=%fused_computation.66.clone.1 | convolution fusion | flops 1115691008 | bytes 69730304 | tf_op jit(solution)/shard_map/while/body/eval_jaxpr/hqk,khd->qhd/dot_general | solution.py:99
  974.8 43.4 %bitcast_add_fusion.5 = f32[2048,8,64]{0,2,1:T(8,128)} fusion(f32[2048,8,64]{0,2,1:T(8,128)} %get-tuple-element.529, f32[8,512,2048]{2,1,0:T(8,128)} %subtract_exponential_fusion.4, f32[8,512,2048]{2,1,0:T(8,128)} %fusion.335, pred[]{:T(512)S(6)} %compare.3, bf16[2048,8,64]{0,2,1:T(8,128)(2,1)} %get-tuple-element.548, s32[]{:T(128)S(6)} %select_n.138), kind=kOutput, calls=%fused_computation.63.clone.1 | convolution fusion | flops 1117788160 | bytes 143130624 | tf_op jit(solution)/shard_map/while/body/eval_jaxpr/hqk,qhd->khd/dot_general | solution.py:102
  1090.7 42.6 %fusion.336 = bf16[1,512,8,64]{1,3,2,0:T(8,128)(2,1)S(1)} fusion(bf16[2048,8,64]{0,2,1:T(8,128)(2,1)} %get-tuple-element.550, f32[8,512,2048]{2,1,0:T(8,128)} %subtract_exponential_fusion.4, f32[8,512,2048]{2,1,0:T(8,128)} %fusion.335), kind=kOutput, calls=%fused_computation.66.clone.1 | convolution fusion | flops 1115691008 | bytes 69730304 | tf_op jit(solution)/shard_map/while/body/eval_jaxpr/hqk,khd->qhd/dot_general | solution.py:99
  1133.3 44.6 %bitcast_add_fusion.5 = f32[2048,8,64]{0,2,1:T(8,128)} fusion(f32[2048,8,64]{0,2,1:T(8,128)} %get-tuple-element.529, f32[8,512,2048]{2,1,0:T(8,128)} %subtract_exponential_fusion.4, f32[8,512,2048]{2,1,0:T(8,128)} %fusion.335, pred[]{:T(512)S(6)} %compare.3, bf16[2048,8,64]{0,2,1:T(8,128)(2,1)} %get-tuple-element.548, s32[]{:T(128)S(6)} %select_n.138), kind=kOutput, calls=%fused_computation.63.clone.1 | convolution fusion | flops 1117788160 | bytes 143130624 | tf_op jit(solution)/shard_map/while/body/eval_jaxpr/hqk,qhd->khd/dot_general | solution.py:102
  1250.4 42.6 %fusion.336 = bf16[1,512,8,64]{1,3,2,0:T(8,128)(2,1)S(1)} fusion(bf16[2048,8,64]{0,2,1:T(8,128)(2,1)} %get-tuple-element.550, f32[8,512,2048]{2,1,0:T(8,128)} %subtract_exponential_fusion.4, f32[8,512,2048]{2,1,0:T(8,128)} %fusion.335), kind=kOutput, calls=%fused_computation.66.clone.1 | convolution fusion | flops 1115691008 | bytes 69730304 | tf_op jit(solution)/shard_map/while/body/eval_jaxpr/hqk,khd->qhd/dot_general | solution.py:99
  1293.0 44.6 %bitcast_add_fusion.5 = f32[2048,8,64]{0,2,1:T(8,128)} fusion(f32[2048,8,64]{0,2,1:T(8,128)} %get-tuple-element.529, f32[8,512,2048]{2,1,0:T(8,128)} %subtract_exponential_fusion.4, f32[8,512,2048]{2,1,0:T(8,128)} %fusion.335, pred[]{:T(512)S(6)} %compare.3, bf16[2048,8,64]{0,2,1:T(8,128)(2,1)} %get-tuple-element.548, s32[]{:T(128)S(6)} %select_n.138), kind=kOutput, calls=%fused_computation.63.clone.1 | convolution fusion | flops 1117788160 | bytes 143130624 | tf_op jit(solution)/shard_map/while/body/eval_jaxpr/hqk,qhd->khd/dot_general | solution.py:102
  1410.2 42.6 %fusion.336 = bf16[1,512,8,64]{1,3,2,0:T(8,128)(2,1)S(1)} fusion(bf16[2048,8,64]{0,2,1:T(8,128)(2,1)} %get-tuple-element.550, f32[8,512,2048]{2,1,0:T(8,128)} %subtract_exponential_fusion.4, f32[8,512,2048]{2,1,0:T(8,128)} %fusion.335), kind=kOutput, calls=%fused_computation.66.clone.1 | convolution fusion | flops 1115691008 | bytes 69730304 | tf_op jit(solution)/shard_map/while/body/eval_jaxpr/hqk,khd->qhd/dot_general | solution.py:99
  1452.8 44.6 %bitcast_add_fusion.5 = f32[2048,8,64]{0,2,1:T(8,128)} fusion(f32[2048,8,64]{0,2,1:T(8,128)} %get-tuple-element.529, f32[8,512,2048]{2,1,0:T(8,128)} %subtract_exponential_fusion.4, f32[8,512,2048]{2,1,0:T(8,128)} %fusion.335, pred[]{:T(512)S(6)} %compare.3, bf16[2048,8,64]{0,2,1:T(8,128)(2,1)} %get-tuple-element.548, s32[]{:T(128)S(6)} %select_n.138), kind=kOutput, calls=%fused_computation.63.clone.1 | convolution fusion | flops 1117788160 | bytes 143130624 | tf_op jit(solution)/shard_map/while/body/eval_jaxpr/hqk,qhd->khd/dot_general | solution.py:102
  1544.8 97.9 %reduce-scatter.28.cloned.1.call-done = f32[1024,1024]{1,0:T(8,128)} async-done(((f32[2048,1024]{1,0:T(8,128)}), f32[1024,1024]{1,0:T(8,128)}) %reduce-scatter.28.cloned.1.call-update) | async-done | bytes 4194320 | tf_op jit(solution)/shard_map/reduce_scatter | solution.py:151
  1701.0 47.1 %all-gather.15.cloned.1.call-done = bf16[2048,1024]{1,0:T(8,128)(2,1)} async-done(((bf16[1024,1024]{1,0:T(8,128)(2,1)}), bf16[2048,1024]{1,0:T(8,128)(2,1)}) %all-gather.15.cloned.1.call-update) | async-done | bytes 4194320 | tf_op jit(solution)/shard_map/all_gather | solution.py:130
  1763.6 144.7 %while.37 = (s32[]{:T(128)}, bf16[4,512,512]{2,1,0:T(8,128)(2,1)}, s32[4]{0:T(128)S(1)}, s32[1,2]{1,0:T(1,128)S(1)}, bf16[2048,8,64]{0,2,1:T(8,128)(2,1)}, /*ind...) while((s32[]{:T(128)}, bf16[4,512,512]{2,1,0:T(8,128)(2,1)}, ...), condition=%wide.region_7.8_spmd, body=%wide.region_2.7_spmd.sunk | while | flops 2202297856 | bytes 76608768 | solution.py:78
  1921.5 101.7 %reduce-scatter.12.cloned.1.call-done = f32[1024,1024]{1,0:T(8,128)} async-done(((f32[2048,1024]{1,0:T(8,128)}), f32[1024,1024]{1,0:T(8,128)}) %reduce-scatter.12.cloned.1.call-update) | async-done | bytes 4194320 | tf_op jit(solution)/shard_map/reduce_scatter | solution.py:137
  2075.9 57.3 %all-gather.21.cloned.1.call-done = bf16[2048,1024]{1,0:T(8,128)(2,1)} async-done(((bf16[1024,1024]{1,0:T(8,128)(2,1)}), bf16[2048,1024]{1,0:T(8,128)(2,1)}) %all-gather.21.cloned.1.call-update) | async-done | bytes 4194320 | tf_op jit(solution)/shard_map/all_gather | solution.py:130
  2209.9 88.5 %all-reduce.7.cloned.1.call-done = (bf16[8,16,3,512]{3,1,2,0:T(8,128)(2,1)}, bf16[8,512,16]{1,2,0:T(8,128)(2,1)}, bf16[8,16,2048]{2,1,0:T(8,128)(2,1)}, bf16[8,2048,16]{1,2,0:T(8,128)(2,1)}) async-done(((bf16[8,16,3,512]{3,1,2,0:T(8,128)(2,1)}, bf16[8,512,16]{1,2,0:T(8,128)(2,1)}, bf16[8,16,2048]{2,1,0:T(8,128)(2,1)}, bf16[8,2048,16]{1,2,0:T(8,128)(2,1)}), (bf16[8,16,3,512]{3,1,2,0:T(8,128)(2,1)}, ...) | async-done | bytes 1572880 | tf_op jit(solution)/shard_map/psum | solution.py:322
  2310.3 101.4 %reduce-scatter.16.cloned.1.call-done = f32[1024,1024]{1,0:T(8,128)} async-done(((f32[2048,1024]{1,0:T(8,128)}), f32[1024,1024]{1,0:T(8,128)}) %reduce-scatter.16.cloned.1.call-update) | async-done | bytes 4194320 | tf_op jit(solution)/shard_map/reduce_scatter | solution.py:137
  2417.3 136.9 %all-reduce.5.cloned.1.call-done = (f32[8,1024,16]{1,2,0:T(8,128)}, f32[8,16,1024]{2,1,0:T(8,128)}, f32[8,1024,16]{1,2,0:T(8,128)}, f32[8,16,1024]{2,1,0:T(8,128)}) async-done(((f32[8,1024,16]{1,2,0:T(8,128)}, f32[8,16,1024]{2,1,0:T(8,128)}, f32[8,1024,16]{1,2,0:T(8,128)}, f32[8,16,1024]{2,1,0:T(8,128)}), (f32[8,1024,16]{1,2,0:T(8,128)}, f32[8,16,1024]{2,1,0:T(8,128)}, f32[8,1024,16]{1,2,0:T(8,128)}, ...) | async-done | bytes 2097168 | tf_op jit(solution)/shard_map/psum | solution.py:329
  (424 shorter events, 1146.8 us)
Async XLA Ops:
  14.5 316.2 %all-gather.35.cloned.1.call-start = ((), (), s32[]{:S(2)}) async-start(), calls=%async_computation.25 | async-start | bytes 1114112 | tf_op jit(solution)/shard_map/all_gather | solution.py:124
  15.3 326.0 %reduce-scatter.22.cloned.1.call-start = ((), (), s32[]{:S(2)}) async-start(), calls=%async_computation.27 | async-start | bytes 196608 | tf_op jit(solution)/shard_map/reduce_scatter | solution.py:138
  330.7 111.9 %reduce-scatter.20.cloned.1.call-start = ((), (), s32[]{:S(2)}) async-start(), calls=%async_computation.26 | async-start | bytes 12582912 | tf_op jit(solution)/shard_map/reduce_scatter | solution.py:137
  338.3 157.1 %all-gather.39.cloned.1.call-start = ((), (), s32[]{:S(2)}) async-start(), calls=%async_computation.29 | async-start | bytes 4456448 | tf_op jit(solution)/shard_map/all_gather | solution.py:123
  338.9 213.5 %all-gather.37.cloned.1.call-start = ((), (), s32[]{:S(2)}) async-start(), calls=%async_computation.28 | async-start | bytes 6291456 | tf_op jit(solution)/shard_map/all_gather | solution.py:130
  449.8 161.0 %all-gather.29.cloned.1.call-start = ((), (), s32[]{:S(2)}) async-start(), calls=%async_computation.22 | async-start | bytes 6291456 | tf_op jit(solution)/shard_map/all_gather | solution.py:144
  450.6 213.2 %all-gather.27.cloned.1.call-start = ((), (), s32[]{:S(2)}) async-start(), calls=%async_computation.21 | async-start | bytes 4456448 | tf_op jit(solution)/shard_map/all_gather | solution.py:124
  451.3 257.8 %reduce-scatter.26.cloned.1.call-start = ((), (), s32[]{:S(2)}) async-start(), calls=%async_computation.31 | async-start | bytes 196608 | tf_op jit(solution)/shard_map/reduce_scatter | solution.py:152
  694.4 112.6 %reduce-scatter.24.cloned.1.call-start = ((), (), s32[]{:S(2)}) async-start(), calls=%async_computation.30 | async-start | bytes 12582912 | tf_op jit(solution)/shard_map/reduce_scatter | solution.py:151
  709.0 165.2 %all-gather.41.cloned.1.call-start = ((), (), s32[]{:S(2)}) async-start(), calls=%async_computation.32 | async-start | bytes 6291456 | tf_op jit(solution)/shard_map/all_gather | solution.py:144
  817.3 727.5 %reduce-scatter.30.cloned.1.call-start = ((), (), s32[]{:S(2)}) async-start(), calls=%async_computation.34 | async-start | bytes 196608 | tf_op jit(solution)/shard_map/reduce_scatter | solution.py:152
  1542.9 147.4 %all-gather.17.cloned.1.call-start = ((), (), s32[]{:S(2)}) async-start(), calls=%async_computation.12 | async-start | bytes 3342336 | tf_op jit(solution)/shard_map/all_gather | solution.py:123
  1543.5 204.6 %all-gather.15.cloned.1.call-start = ((), (), s32[]{:S(2)}) async-start(), calls=%async_computation.11 | async-start | bytes 6291456 | tf_op jit(solution)/shard_map/all_gather | solution.py:130
  1653.3 258.0 %all-gather.19.cloned.1.call-start = ((), (), s32[]{:S(2)}) async-start(), calls=%async_computation.13 | async-start | bytes 1114112 | tf_op jit(solution)/shard_map/all_gather | solution.py:124
  1653.9 267.6 %reduce-scatter.14.cloned.1.call-start = ((), (), s32[]{:S(2)}) async-start(), calls=%async_computation.15 | async-start | bytes 196608 | tf_op jit(solution)/shard_map/reduce_scatter | solution.py:138
  1911.2 111.9 %reduce-scatter.12.cloned.1.call-start = ((), (), s32[]{:S(2)}) async-start(), calls=%async_computation.14 | async-start | bytes 12582912 | tf_op jit(solution)/shard_map/reduce_scatter | solution.py:137
  1918.9 157.0 %all-gather.23.cloned.1.call-start = ((), (), s32[]{:S(2)}) async-start(), calls=%async_computation.17 | async-start | bytes 4456448 | tf_op jit(solution)/shard_map/all_gather | solution.py:123
  1919.5 213.7 %all-gather.21.cloned.1.call-start = ((), (), s32[]{:S(2)}) async-start(), calls=%async_computation.16 | async-start | bytes 6291456 | tf_op jit(solution)/shard_map/all_gather | solution.py:130
  2030.3 155.6 %all-gather.25.cloned.1.call-start = ((), (), s32[]{:S(2)}) async-start(), calls=%async_computation.18 | async-start | bytes 4456448 | tf_op jit(solution)/shard_map/all_gather | solution.py:124
  2031.1 169.5 %reduce-scatter.32.cloned.1.call-start = ((), (), s32[]{:S(2)}) async-start(), calls=%async_computation.35 | async-start | bytes 196608 | tf_op jit(solution)/shard_map/reduce_scatter | solution.py:138
  2049.4 249.0 %all-reduce.7.cloned.1.call-start = ((), (), s32[]{:S(2)}) async-start(), calls=%async_computation.37 | async-start | bytes 3145728 | tf_op jit(solution)/shard_map/psum | solution.py:322
  2058.0 252.3 %reduce-scatter.18.cloned.1.call-start = ((), (), s32[]{:S(2)}) async-start(), calls=%async_computation.20 | async-start | bytes 196608 | tf_op jit(solution)/shard_map/reduce_scatter | solution.py:138
  2165.1 246.6 %reduce-scatter.16.cloned.1.call-start = ((), (), s32[]{:S(2)}) async-start(), calls=%async_computation.19 | async-start | bytes 12582912 | tf_op jit(solution)/shard_map/reduce_scatter | solution.py:137
  2200.6 353.6 %all-reduce.5.cloned.1.call-start = ((), (), s32[]{:S(2)}) async-start(), calls=%async_computation.36 | async-start | bytes 4194304 | tf_op jit(solution)/shard_map/psum | solution.py:329
  (52 other events, 1760.8 us)
Sparse Core Ops, SparseCore 0:
  10.2 48.1 all-gather.32
  60.0 55.5 all-gather.30
  117.7 37.9 all-gather.34
  330.8 10.3 reduce-scatter.21
  343.4 99.2 reduce-scatter.19
  444.9 50.5 all-gather.38
  497.1 55.2 all-gather.36
  554.0 56.7 all-gather.28
  613.2 50.5 all-gather.26
  709.2 97.7 reduce-scatter.23
  817.4 56.7 all-gather.40
  1531.0 10.2 reduce-scatter.29
  1543.5 99.2 reduce-scatter.27
  1645.0 45.2 all-gather.16
  1692.3 55.6 all-gather.14
  1750.3 37.8 all-gather.18
  1911.4 10.1 reduce-scatter.13
  1923.9 99.2 reduce-scatter.11
  2025.2 50.6 all-gather.22
  2078.0 55.1 all-gather.20
  2135.3 50.5 all-gather.24
  2202.3 96.0 all-reduce.6
  2312.4 99.2 reduce-scatter.15
  2419.3 134.7 all-reduce.4
  (3 shorter events, 26.4 us)
where the time goes:
time: 2580 us; the launch traced here: 2570 us
  waiting for transfers between devices  1200 us (47%)
  matrix products  1030 us (40%)
  local copies, waits for them, and re-layouts  148 us (6%)
  other arithmetic  123 us (5%)
  blocking collectives  28.6 us (1%)
    reduce_scatter x3, waiting for transfers between devices, leave_rows(): lax.psum_scatter(partial_value, 'tensor', scatter_dimension=0, tiled=True)  305 us
    all_gather x4, waiting for transfers between devices, enter_rows(): lax.all_gather(normed, 'tensor', axis=0, tiled=True)  214 us
    reduce_scatter x2, waiting for transfers between devices, leave_grads(): lax.psum_scatter(partial_value, 'tensor', scatter_dimension=0, tiled=True)  196 us
    dot_general x4, matrix products, one_block(): jnp.einsum('hqk,qhd->khd', slopes, query_block, preferred_element_type=jn...  177 us
    dot_general x4, matrix products, one_block(): jnp.einsum('hqk,khd->qhd', slopes, key_rows, preferred_element_type=jnp.f...  170 us
    dot_general x22, matrix products, matmul(): return jnp.dot(left, right, preferred_element_type=jnp.float32)  141 us
    psum x1, waiting for transfers between devices, per_device(): lax.psum((spread(grad_a_qkv_here, 0), spread(grad_b_out_here, 1), spread(...  137 us
    dot_general x8, matrix products, masked_scores(): jnp.einsum('qhd,khd->hqk', query_block, key_rows, preferred_element_type=...  129 us
  transfers between devices with their start and end apart: 27, of which 22 were waited for; matrix products, arithmetic and copies ran while one was open for 23% of the time, Pallas kernels for 0%

commit v1 on v0

--- a/solution.py
+++ b/solution.py
@@ -1,6 +1,11 @@
+import functools
+import math
+
 import jax
 import jax.numpy as jnp
 from jax import lax
+from jax.experimental import pallas as pl
+from jax.experimental.pallas import tpu as pltpu
 from jax.sharding import PartitionSpec as P
 
 HD = 64
@@ -240,8 +245,6 @@
 
     frozen = (w_qkv, w_out, w_up, w_down)
     output, kept_state = run_forward(tokens, frozen)
-    fresh_tokens, fresh_frozen = lax.optimization_barrier((tokens, frozen))
-    repeat_out, kept_state = run_forward(fresh_tokens, fresh_frozen)
     (
         qkv_flat,
         out_full,
@@ -349,6 +352,711 @@
     )
 
 
+LOG2E = math.log2(math.e)
+MASKED = -1e30
+MIB = 1 << 20
+BF = jnp.bfloat16
+F32 = jnp.float32
+
+
+def nt(a, b):
+    return lax.dot_general(a, b, (((1,), (1,)), ((), ())), preferred_element_type=F32)
+
+
+def nn(a, b):
+    return lax.dot_general(a, b, (((1,), (0,)), ((), ())), preferred_element_type=F32)
+
+
+def tn(a, b):
+    return lax.dot_general(a, b, (((0,), (0,)), ((), ())), preferred_element_type=F32)
+
+
+def last_key(starts_ref, pos):
+    lim = pos
+    for n in range(starts_ref.shape[0]):
+        first = starts_ref[n]
+        lim = jnp.where((pos >= first) & (pos < first + SPAN), first + SPAN - 1, lim)
+    return lim
+
+
+def head_parts(x):
+    lane = lax.broadcasted_iota(jnp.int32, x.shape, 1)
+    zero = jnp.zeros_like(x)
+    return jnp.where(lane < HD, x, zero), jnp.where(lane >= HD, x, zero)
+
+
+def attend_kernel(bq, starts_ref, q_ref, k_ref, v_ref, o_ref, lse_ref, vt_ref):
+    qi = pl.program_id(1)
+    bk = k_ref.shape[1]
+    scale = LOG2E * HD ** -0.5
+
+    @pl.when(qi == 0)
+    def _():
+        for n in range(k_ref.shape[0]):
+            vt_ref[:, n * bk : (n + 1) * bk] = jnp.transpose(v_ref[n])
+
+    qs = head_parts(q_ref[...])
+    base = qi * bq
+    lim = last_key(starts_ref, base + lax.broadcasted_iota(jnp.int32, (1, bq), 1))
+    last = last_key(starts_ref, base + bq - 1)
+
+    def step(masked, j, carry):
+        off = pl.multiple_of(j * bk, bk)
+        keys = k_ref[j]
+        out = []
+        for h in range(2):
+            m, l, acc = carry[h]
+            s = nt(keys, qs[h])
+            if masked:
+                kpos = off + lax.broadcasted_iota(jnp.int32, (bk, bq), 0)
+                s = jnp.where(kpos <= lim, s, MASKED)
+            mn = jnp.maximum(m, jnp.max(s, axis=0, keepdims=True))
+            p = jnp.exp2((s - mn) * scale)
+            al = jnp.exp2((m - mn) * scale)
+            l = al * l + jnp.sum(p, axis=0, keepdims=True)
+            acc = acc * al + nn(vt_ref[h * HD : (h + 1) * HD, pl.ds(off, bk)], p.astype(BF))
+            out.append((mn, l, acc))
+        return tuple(out)
+
+    init = (jnp.full((1, bq), MASKED, F32), jnp.zeros((1, bq), F32), jnp.zeros((HD, bq), F32))
+    carry = lax.fori_loop(0, base // bk, functools.partial(step, False), (init, init))
+    carry = lax.fori_loop(base // bk, last // bk + 1, functools.partial(step, True), carry)
+    mixed = jnp.concatenate([carry[h][2] / carry[h][1] for h in range(2)], axis=0)
+    o_ref[...] = jnp.transpose(mixed).astype(BF)
+    for h in range(2):
+        lse_ref[0, h : h + 1, :] = carry[h][0] * scale + jnp.log2(carry[h][1])
+
+
+def attend_rows(starts, qkv):
+    parts, _, rows, width = qkv.shape
+    pairs = width // (2 * HD)
+    length = parts * rows
+    bq = rows
+
+    def all_parts(which):
+        return pl.BlockSpec((parts, None, rows, 2 * HD), lambda p, i, s: (0, which, 0, p))
+
+    return pl.pallas_call(
+        functools.partial(attend_kernel, bq),
+        out_shape=(
+            jax.ShapeDtypeStruct((parts, rows, width), BF),
+            jax.ShapeDtypeStruct((pairs, 2, length), F32),
+        ),
+        grid_spec=pltpu.PrefetchScalarGridSpec(
+            num_scalar_prefetch=1,
+            grid=(pairs, parts),
+            in_specs=[
+                pl.BlockSpec((None, None, rows, 2 * HD), lambda p, i, s: (i, 0, 0, p)),
+                all_parts(1),
+                all_parts(2),
+            ],
+            out_specs=[
+                pl.BlockSpec((None, rows, 2 * HD), lambda p, i, s: (i, 0, p)),
+                pl.BlockSpec((1, 2, rows), lambda p, i, s: (p, 0, i)),
+            ],
+            scratch_shapes=[pltpu.VMEM((2 * HD, length), BF)],
+        ),
+        compiler_params=pltpu.CompilerParams(
+            dimension_semantics=("arbitrary", "arbitrary"), vmem_limit_bytes=48 * MIB
+        ),
+        name="attend",
+    )(starts, qkv, qkv, qkv)
+
+
+def attend_back_kernel(
+    bq, bk, starts_ref, q_ref, k_ref, v_ref, o_ref, do_ref, lse_ref, g_ref,
+    kt_ref, dqt_ref, delta_ref, qm_ref, dom_ref,
+):
+    parts, rows, _ = q_ref.shape
+    length = parts * rows
+    scale = LOG2E * HD ** -0.5
+    nq = length // bq
+    per = rows // bq
+    dqt_ref[...] = jnp.zeros_like(dqt_ref)
+    for i in range(nq):
+        part, at = i // per, slice((i % per) * bq, (i % per + 1) * bq)
+        flat = slice(i * bq, (i + 1) * bq)
+        kt_ref[:, flat] = jnp.transpose(k_ref[part, at, :])
+        do = do_ref[part, at, :]
+        for h, (q_h, do_h) in enumerate(zip(head_parts(q_ref[part, at, :]), head_parts(do))):
+            qm_ref[h, flat, :] = q_h
+            dom_ref[h, flat, :] = do_h
+        prod = jnp.transpose(do.astype(F32) * o_ref[part, at, :].astype(F32))
+        for h in range(2):
+            delta_ref[h : h + 1, flat] = jnp.sum(prod[h * HD : (h + 1) * HD], axis=0, keepdims=True)
+
+    @pl.loop(0, length // bk)
+    def _(j):
+        koff = pl.multiple_of(j * bk, bk)
+        part = j // (rows // bk)
+        inside = pl.multiple_of((j % (rows // bk)) * bk, bk)
+        keys = k_ref[part, pl.ds(inside, bk), :]
+        vals = v_ref[part, pl.ds(inside, bk), :]
+
+        def step(masked, i, carry):
+            dk, dv = carry
+            at = pl.ds(pl.multiple_of(i * bq, bq), bq)
+            if masked:
+                lim = last_key(starts_ref, i * bq + lax.broadcasted_iota(jnp.int32, (1, bq), 1))
+                kpos = koff + lax.broadcasted_iota(jnp.int32, (bk, bq), 0)
+                ok = kpos <= lim
+            for h in range(2):
+                q_h = qm_ref[h, at, :]
+                do_h = dom_ref[h, at, :]
+                p = jnp.exp2(nt(keys, q_h) * scale - lse_ref[0, h : h + 1, at])
+                if masked:
+                    p = jnp.where(ok, p, 0.0)
+                dp = nt(vals, do_h)
+                ds = (p * (dp - delta_ref[h : h + 1, at])).astype(BF)
+                dv = dv + nn(p.astype(BF), do_h)
+                dk = dk + nn(ds, q_h)
+                dqt_ref[h * HD : (h + 1) * HD, at] += nn(
+                    kt_ref[h * HD : (h + 1) * HD, pl.ds(koff, bk)], ds
+                )
+            return dk, dv
+
+        first_q = koff
+        for n in range(starts_ref.shape[0]):
+            first = starts_ref[n]
+            here = (koff >= first) & (koff < first + SPAN)
+            first_q = jnp.where(here, jnp.minimum(first_q, first), first_q)
+        full = (koff + bk + bq - 2) // bq
+        zero = jnp.zeros((bk, 2 * HD), F32)
+        carry = lax.fori_loop(first_q // bq, full, functools.partial(step, True), (zero, zero))
+        dk, dv = lax.fori_loop(full, nq, functools.partial(step, False), carry)
+        g_ref[part, 1, pl.ds(inside, bk), :] = (dk * HD ** -0.5).astype(BF)
+        g_ref[part, 2, pl.ds(inside, bk), :] = dv.astype(BF)
+
+    for i in range(nq):
+        part, at = i // per, slice((i % per) * bq, (i % per + 1) * bq)
+        dq = jnp.transpose(dqt_ref[:, i * bq : (i + 1) * bq])
+        g_ref[part, 0, at, :] = (dq * HD ** -0.5).astype(BF)
+
+
+def attend_rows_back(starts, qkv, mixed, grad_mix, lse):
+    parts, _, rows, width = qkv.shape
+    pairs = width // (2 * HD)
+    length = parts * rows
+    bq = bk = min(512, rows)
+
+    def one(which):
+        return pl.BlockSpec((parts, None, rows, 2 * HD), lambda p, s: (0, which, 0, p))
+
+    flat = pl.BlockSpec((parts, rows, 2 * HD), lambda p, s: (0, 0, p))
+    return pl.pallas_call(
+        functools.partial(attend_back_kernel, bq, bk),
+        out_shape=jax.ShapeDtypeStruct((parts, 3, rows, width), BF),
+        grid_spec=pltpu.PrefetchScalarGridSpec(
+            num_scalar_prefetch=1,
+            grid=(pairs,),
+            in_specs=[one(0), one(1), one(2), flat, flat,
+                      pl.BlockSpec((1, 2, length), lambda p, s: (p, 0, 0))],
+            out_specs=pl.BlockSpec((parts, 3, rows, 2 * HD), lambda p, s: (0, 0, 0, p)),
+            scratch_shapes=[
+                pltpu.VMEM((2 * HD, length), BF),
+                pltpu.VMEM((2 * HD, length), F32),
+                pltpu.VMEM((2, length), F32),
+                pltpu.VMEM((2, length, 2 * HD), BF),
+                pltpu.VMEM((2, length, 2 * HD), BF),
+            ],
+        ),
+        compiler_params=pltpu.CompilerParams(
+            dimension_semantics=("arbitrary",), vmem_limit_bytes=48 * MIB
+        ),
+        name="attend_back",
+    )(starts, qkv, qkv, qkv, mixed, grad_mix, lse)
+
+
+def stats(x):
+    center = x - jnp.mean(x, axis=-1, keepdims=True)
+    return center, lax.rsqrt(jnp.mean(center * center, axis=-1, keepdims=True) + 1e-05)
+
+
+def norm_back(x, gain, grad):
+    center, r = stats(x)
+    n = center * r
+    e = grad * gain
+    return r * (e - jnp.mean(e, axis=-1, keepdims=True) - n * jnp.mean(e * n, axis=-1, keepdims=True))
+
+
+def row_loop(rows, chunk, body):
+    @pl.loop(0, rows // chunk)
+    def _(i):
+        body(pl.ds(pl.multiple_of(i * chunk, chunk), chunk))
+
+
+def qkv_kernel(tok_ref, gain_ref, bias_ref, low_in_ref, w_ref, low_up_ref, out_ref, norm_ref, low_ref):
+    rows = tok_ref.shape[0]
+    first = (pl.program_id(0) == 0) & (pl.program_id(1) == 0)
+
+    @pl.when(first)
+    def _():
+        def body(at):
+            center, r = stats(tok_ref[at, :].astype(F32))
+            normed = (center * r * gain_ref[...] + bias_ref[...]).astype(BF)
+            norm_ref[at, :] = normed
+            low_ref[at, :] = nt(normed, low_in_ref[...]).astype(BF)
+
+        row_loop(rows, 256, body)
+
+    w = w_ref[...].reshape(norm_ref.shape[1], -1)
+
+    def body(at):
+        y = nn(norm_ref[at, :], w) + nn(low_ref[at, :], low_up_ref[...])
+        out_ref[at, :] = y.astype(BF)
+
+    row_loop(rows, 512, body)
+
+
+def whole(shape):
+    return pl.BlockSpec(shape, lambda *_: (0,) * len(shape))
+
+
+def project_qkv(tok, gain, bias, low_in, w, low_up):
+    rows, features = tok.shape
+    shards, groups, _, part, width = w.shape
+    rank = low_in.shape[0]
+    return pl.pallas_call(
+        qkv_kernel,
+        out_shape=(
+            jax.ShapeDtypeStruct((groups, 3, rows, width), BF),
+            jax.ShapeDtypeStruct((rows, features), BF),
+            jax.ShapeDtypeStruct((rows, rank), BF),
+        ),
+        grid=(groups, 3),
+        in_specs=[
+            whole((rows, features)), whole((1, features)), whole((1, features)),
+            whole((rank, features)),
+            pl.BlockSpec((shards, None, None, part, width), lambda g, j: (0, g, j, 0, 0)),
+            pl.BlockSpec((None, rank, width), lambda g, j: (g, 0, j)),
+        ],
+        out_specs=[
+            pl.BlockSpec((None, None, rows, width), lambda g, j: (g, j, 0, 0)),
+            whole((rows, features)),
+            whole((rows, rank)),
+        ],
+        compiler_params=pltpu.CompilerParams(
+            dimension_semantics=("arbitrary", "arbitrary"), vmem_limit_bytes=48 * MIB
+        ),
+        name="project_qkv",
+    )(tok, gain, bias, low_in, w, low_up)
+
+
+def qkv_back_kernel(
+    g_ref, w_ref, low_up_ref, low_in_ref, norm_ref, low_ref, tok_ref, gain_ref, resid_ref,
+    grad_ref, gb_ref, ga_ref, acc_ref, glow_ref,
+):
+    rows = tok_ref.shape[0]
+    g, j = pl.program_id(0), pl.program_id(1)
+    first = (g == 0) & (j == 0)
+    final = (g == pl.num_programs(0) - 1) & (j == pl.num_programs(1) - 1)
+    w = w_ref[...].reshape(tok_ref.shape[1], -1)
+
+    @pl.when(first)
+    def _():
+        acc_ref[...] = jnp.zeros_like(acc_ref)
+        glow_ref[...] = jnp.zeros_like(glow_ref)
+
+    def body(at):
+        part = g_ref[at, :]
+        acc_ref[at, :] += nt(part, w)
+        glow_ref[at, :] += nt(part, low_up_ref[...])
+
+    row_loop(rows, 512, body)
+    gb_ref[...] = tn(low_ref[...], g_ref[...]).astype(gb_ref.dtype)
+
+    @pl.when(final)
+    def _():
+        def body(at):
+            glow = glow_ref[at, :].astype(BF)
+            total = acc_ref[at, :] + nn(glow, low_in_ref[...])
+            grad_ref[at, :] = resid_ref[at, :] + norm_back(
+                tok_ref[at, :].astype(F32), gain_ref[...], total
+            )
+
+        row_loop(rows, 256, body)
+        ga_ref[...] = tn(glow_ref[...].astype(BF), norm_ref[...]).astype(ga_ref.dtype)
+
+
+def project_qkv_back(grad, w, low_up, low_in, normed, low, tok, gain, resid):
+    rows, features = tok.shape
+    shards, groups, _, part, width = w.shape
+    rank = low_in.shape[0]
+    return pl.pallas_call(
+        qkv_back_kernel,
+        out_shape=(
+            jax.ShapeDtypeStruct((rows, features), F32),
+            jax.ShapeDtypeStruct((rank, groups * 3 * width), BF),
+            jax.ShapeDtypeStruct((rank, features), BF),
+        ),
+        grid=(groups, 3),
+        in_specs=[
+            pl.BlockSpec((None, None, rows, width), lambda g, j: (g, j, 0, 0)),
+            pl.BlockSpec((shards, None, None, part, width), lambda g, j: (0, g, j, 0, 0)),
+            pl.BlockSpec((None, rank, width), lambda g, j: (g, 0, j)),
+            whole((rank, features)), whole((rows, features)), whole((rows, rank)),
+            whole((rows, features)), whole((1, features)), whole((rows, features)),
+        ],
+        out_specs=[
+            whole((rows, features)),
+            pl.BlockSpec((rank, width), lambda g, j: (0, g * 3 + j)),
+            whole((rank, features)),
+        ],
+        scratch_shapes=[pltpu.VMEM((rows, features), F32), pltpu.VMEM((rows, rank), F32)],
+        compiler_params=pltpu.CompilerParams(
+            dimension_semantics=("arbitrary", "arbitrary"), vmem_limit_bytes=56 * MIB
+        ),
+        name="project_qkv_back",
+    )(grad, w, low_up, low_in, normed, low, tok, gain, resid)
+
+
+GELU = math.sqrt(2.0 / math.pi)
+
+
+def gelu_and_slope(v):
+    v2 = v * v
+    t = jnp.tanh(GELU * v * (1.0 + 0.044715 * v2))
+    half = 0.5 * (1.0 + t)
+    return v * half, half + 0.5 * v * (1.0 - t * t) * (GELU * (1.0 + 3 * 0.044715 * v2))
+
+
+def middle_kernel(
+    nf, tt_ref, cc_ref, sc_ref, w_ref, sh_ref, tok_ref, mix_ref, cot_ref, gain_ref, bias_ref, rep_ref,
+    out_ref, resid_ref, gmix_ref, gr_ref, lo_ref,
+    acc_ref, norm_ref, hid_ref, slope_ref, lacc_ref, llow_ref,
+):
+    rows, features = tok_ref.shape
+    s = pl.program_id(0)
+    w = w_ref[...].reshape(features, -1)
+    c = w.shape[1]
+    sh = sh_ref[...]
+    b_out, a_up, b_down = rep_ref[0], rep_ref[1], rep_ref[2]
+    chunk = 512
+    up0, down0, upb0, end0 = 2, 2 + nf, 2 + 2 * nf, 2 + 3 * nf
+
+    @pl.when(s < up0)
+    def _():
+        def body(at):
+            part = mix_ref[s, at, :]
+            y = nt(part, w)
+            low = nt(part, sh)
+
+            @pl.when(s == 0)
+            def _():
+                resid_ref[at, :] = tok_ref[at, :].astype(F32) + y
+                lacc_ref[at, :] = low
+
+            @pl.when(s > 0)
+            def _():
+                resid_ref[at, :] += y
+                lacc_ref[at, :] += low
+
+        row_loop(rows, chunk, body)
+
+    @pl.when(s == up0 - 1)
+    def _():
+        def body(at):
+            low = lacc_ref[at, :].astype(BF)
+            llow_ref[0, at, :] = low
+            resid = resid_ref[at, :] + nn(low, b_out)
+            resid_ref[at, :] = resid
+            center, r = stats(resid)
+            normed = (center * r * gain_ref[...] + bias_ref[...]).astype(BF)
+            norm_ref[at, :] = normed
+            llow_ref[1, at, :] = nt(normed, a_up).astype(BF)
+            llow_ref[3, at, :] = nt(cot_ref[at, :], b_down).astype(BF)
+
+        row_loop(rows, 256, body)
+
+    @pl.when((s >= up0) & (s < down0))
+    def _():
+        f = s - up0
+
+        def body(at):
+            pre = nn(norm_ref[at, :], w) + nn(llow_ref[1, at, :], sh)
+            hidden, slope = gelu_and_slope(pre)
+            hid_ref[f, at, :] = hidden.astype(BF)
+            slope_ref[f, at, :] = slope.astype(BF)
+
+        row_loop(rows, 256, body)
+
+    @pl.when((s >= down0) & (s < upb0))
+    def _():
+        f = s - down0
+
+        def body(at):
+            hidden = hid_ref[f, at, :]
+            y = nt(hidden, w)
+            low = nt(hidden, sh)
+
+            @pl.when(f == 0)
+            def _():
+                acc_ref[at, :] = y
+                lacc_ref[at, :] = low
+
+            @pl.when(f > 0)
+            def _():
+                acc_ref[at, :] += y
+                lacc_ref[at, :] += low
+
+            g_hidden = nn(cot_ref[at, :], w) + nn(llow_ref[3, at, :], sh)
+            slope_ref[f, at, :] = (g_hidden * slope_ref[f, at, :].astype(F32)).astype(BF)
+
+        row_loop(rows, chunk, body)
+        gr_ref[0:16, :] = tn(llow_ref[3], hid_ref[f]).astype(gr_ref.dtype)
+        gr_ref[16:32, :] = tn(llow_ref[1], slope_ref[f]).astype(gr_ref.dtype)
+
+    @pl.when(s == upb0 - 1)
+    def _():
+        def body(at):
+            low = lacc_ref[at, :].astype(BF)
+            llow_ref[2, at, :] = low
+            out_ref[at, :] = (resid_ref[at, :] + acc_ref[at, :] + nn(low, b_down)).astype(BF)
+
+        row_loop(rows, chunk, body)
+        lo_ref[2] = tn(llow_ref[2], cot_ref[...]).astype(lo_ref.dtype)
+
+    @pl.when((s >= upb0) & (s < end0))
+    def _():
+        f = s - upb0
+
+        def body(at):
+            part = slope_ref[f, at, :]
+            y = nt(part, w)
+            low = nt(part, sh)
+
+            @pl.when(f == 0)
+            def _():
+                acc_ref[at, :] = y
+                lacc_ref[at, :] = low
+
+            @pl.when(f > 0)
+            def _():
+                acc_ref[at, :] += y
+                lacc_ref[at, :] += low
+
+        row_loop(rows, chunk, body)
+
+    @pl.when(s == end0 - 1)
+    def _():
+        llow_ref[4] = lacc_ref[...].astype(BF)
+        lo_ref[1] = tn(llow_ref[4], norm_ref[...]).astype(lo_ref.dtype)
+
+        def body(at):
+            total = acc_ref[at, :] + nn(llow_ref[4, at, :], a_up)
+            g = cot_ref[at, :].astype(F32) + norm_back(resid_ref[at, :], gain_ref[...], total)
+            resid_ref[at, :] = g
+            branch = g.astype(BF)
+            norm_ref[at, :] = branch
+            llow_ref[5, at, :] = nt(branch, b_out).astype(BF)
+
+        row_loop(rows, 256, body)
+        lo_ref[0] = tn(llow_ref[0], norm_ref[...]).astype(lo_ref.dtype)
+
+    @pl.when(s >= end0)
+    def _():
+        g = s - end0
+
+        def body(at):
+            y = nn(norm_ref[at, :], w) + nn(llow_ref[5, at, :], sh)
+            gmix_ref[g, at, :] = y.astype(BF)
+
+        row_loop(rows, chunk, body)
+        gr_ref[0:16, :] = tn(llow_ref[5], mix_ref[g]).astype(gr_ref.dtype)
+
+
+def middle(w, shared, tok, mix, cot, gain, bias, rep):
+    rows, features = tok.shape
+    shards, groups, part, total = w.shape
+    rank = rep.shape[1]
+    c = mix.shape[2]
+    halves = (total // c - 1) // 2
+    nf = groups * halves
+    shift = (shared.shape[2] - total) // c
+    blocks = [(f // halves, f % halves) for f in range(nf)]
+    order = [(g, 0) for g in range(groups)]
+    order += [(t, 1 + h) for t, h in blocks]
+    order += [(t, 1 + halves + h) for t, h in blocks]
+    order += [(t, 1 + h) for t, h in blocks]
+    order += [(g, 0) for g in range(groups)]
+    slot = [0] * (groups + nf) + list(range(nf)) + [nf - 1] * nf + [nf + g for g in range(groups)]
+    tt = jnp.array([t for t, _ in order], jnp.int32)
+    cc = jnp.array([x for _, x in order], jnp.int32)
+    sc = jnp.array(slot, jnp.int32)
+    once = pl.Buffered(1)
+
+    def keep(shape):
+        return pl.BlockSpec(shape, lambda s, *_: (0,) * len(shape), pipeline_mode=once)
+
+    return pl.pallas_call(
+        functools.partial(middle_kernel, nf),
+        out_shape=(
+            jax.ShapeDtypeStruct((rows, features), BF),
+            jax.ShapeDtypeStruct((rows, features), F32),
+            jax.ShapeDtypeStruct(mix.shape, BF),
+            jax.ShapeDtypeStruct((nf + groups, 2 * rank, c), BF),
+            jax.ShapeDtypeStruct((3, rank, features), BF),
+        ),
+        grid_spec=pltpu.PrefetchScalarGridSpec(
+            num_scalar_prefetch=3,
+            grid=(len(order),),
+            in_specs=[
+                pl.BlockSpec((shards, None, part, c), lambda s, tt, cc, sc: (0, tt[s], 0, cc[s])),
+                pl.BlockSpec((None, rank, c), lambda s, tt, cc, sc: (tt[s], 0, cc[s] + shift)),
+                keep((rows, features)), keep(mix.shape), keep((rows, features)),
+                keep((1, features)), keep((1, features)), keep(rep.shape),
+            ],
+            out_specs=[
+                keep((rows, features)), keep((rows, features)), keep(mix.shape),
+                pl.BlockSpec((None, 2 * rank, c), lambda s, tt, cc, sc: (sc[s], 0, 0)),
+                keep((3, rank, features)),
+            ],
+            scratch_shapes=[
+                pltpu.VMEM((rows, features), F32),
+                pltpu.VMEM((rows, features), BF),
+                pltpu.VMEM((nf, rows, c), BF),
+                pltpu.VMEM((nf, rows, c), BF),
+                pltpu.VMEM((rows, rank), F32),
+                pltpu.VMEM((6, rows, rank), BF),
+            ],
+        ),
+        compiler_params=pltpu.CompilerParams(
+            dimension_semantics=("arbitrary",), vmem_limit_bytes=60 * MIB
+        ),
+        name="middle",
+    )(tt, cc, sc, w, shared, tok, mix, cot, gain, bias, rep)
+
+
+def chip_device(
+    tokens, w_qkv, w_out, w_up, w_down, ln1_gain, ln1_bias, ln2_gain, ln2_bias,
+    a_qkv, b_qkv, a_out, b_out, a_up, b_up, a_down, b_down, adapter_idx, pic_start, cotangent,
+):
+    shards = lax.axis_size("dp")
+    dp, t = lax.axis_index("dp"), lax.axis_index("tensor")
+    b = dp % 2
+    stays = b == t
+    cores = [[2 * c, 2 * c + 1] for c in range(shards // 2)]
+    sibling = [(i, i ^ 1) for i in range(shards)]
+    swap = []
+    for c in range(shards // 2):
+        one, two = 2 * (2 * c + 1), 2 * (2 * c) + 1
+        swap += [(one, two), (two, one)]
+
+    def swapped(x):
+        return lax.ppermute(x, ("dp", "tensor"), swap)
+
+    def across(x):
+        return lax.all_to_all(x, "dp", 0, 0, axis_index_groups=cores, tiled=True)
+
+    rows, features = tokens.shape
+    rank = a_qkv.shape[2]
+    tok = jnp.where(stays, tokens, swapped(tokens))
+    cot = jnp.where(stays, cotangent, swapped(cotangent))
+
+    marks = jnp.concatenate([adapter_idx[0], pic_start[0]])
+    other_marks = lax.ppermute(marks, "dp", sibling)
+    mine = jnp.where(stays, marks, other_marks)
+    theirs = jnp.where(stays, other_marks, marks)
+    starts = mine[4:]
+
+    def pick(stacked, which):
+        return lax.dynamic_index_in_dim(stacked, which, 0, keepdims=False)
+
+    def shared_pick(sel):
+        return jnp.concatenate(
+            [
+                pick(b_qkv, sel[0]).reshape(rank, -1),
+                pick(a_out, sel[1]).T,
+                pick(b_up, sel[2]),
+                pick(a_down, sel[3]).T,
+            ],
+            axis=1,
+        )
+
+    own_half = shared_pick(mine)
+    far_half = lax.ppermute(shared_pick(theirs), "tensor", [(0, 1), (1, 0)])
+    shared = jnp.stack([jnp.where(t == 0, own_half, far_half), jnp.where(t == 0, far_half, own_half)])
+    a_qkv_low = pick(a_qkv, mine[0]).T
+    rep = jnp.stack([pick(b_out, mine[1]), pick(a_up, mine[2]).T, pick(b_down, mine[3])])
+
+    part = w_qkv.shape[0]
+    qkv_shard = w_qkv.transpose(1, 0, 2)
+    rest_shard = jnp.concatenate([w_out.T, w_up, w_down.T], axis=1)
+    both = ("dp", "tensor")
+    qkv_full = lax.all_gather(qkv_shard, both, axis=0)
+    qkv_full = qkv_full.reshape(shards, 2, *qkv_shard.shape)
+    rest_full = lax.all_gather(rest_shard, both, axis=0)
+    rest_full = rest_full.reshape(shards, 2, *rest_shard.shape)
+    all_marks = lax.all_gather(adapter_idx[0], "dp", axis=0)
+
+    row = lambda v: v.reshape(1, -1)
+    qkv, normed, low = project_qkv(tok, row(ln1_gain), row(ln1_bias), a_qkv_low, qkv_full, shared)
+    qkv = across(qkv)
+    mixed, lse = attend_rows(starts, qkv)
+    mix = across(mixed)
+    layer_out, g_resid, g_mix, g_blocks, g_rep = middle(
+        rest_full, shared, tok, mix, cot, row(ln2_gain), row(ln2_bias), rep
+    )
+    g_qkv = across(attend_rows_back(starts, qkv, mixed, across(g_mix), lse))
+    grad_tok, g_b_qkv, g_a_qkv = project_qkv_back(
+        g_qkv, qkv_full, shared, a_qkv_low, normed, low, tok, row(ln1_gain), g_resid
+    )
+
+    out = jnp.where(stays, layer_out, swapped(layer_out))
+    grad_input = jnp.where(stays, grad_tok, swapped(grad_tok.astype(BF)).astype(F32))
+
+    slots = a_qkv.shape[0]
+    width = w_qkv.shape[2]
+    ffw = w_up.shape[1]
+    nf = g_blocks.shape[0] - 2
+
+    def total(mine_only, which):
+        seqs = [2 * (d // 2) + u for d in range(shards) for u in range(2)]
+        sel = all_marks[:, which][jnp.array(seqs)]
+        onehot = (jnp.arange(slots, dtype=jnp.int32)[:, None] == sel[None, :]).astype(BF)
+        return lax.dot_general(
+            onehot, mine_only, (((1,), (0,)), ((), ())), preferred_element_type=F32
+        )
+
+    ff = g_blocks[:nf].reshape(nf, 2, rank, -1).transpose(1, 2, 0, 3)
+    g_a_out = g_blocks[nf:, :rank].transpose(1, 0, 2)
+    early_flat = jnp.concatenate(
+        [ff.reshape(-1), g_a_out.reshape(-1), g_rep.reshape(-1)]
+    ).reshape(-1, 1024)
+    early_all = lax.all_gather(early_flat, both, axis=0).reshape(2 * shards, -1)
+    sizes = [rank * 2 * ffw, rank * 2 * ffw, rank * 2 * width, rank * 3 * features]
+    cuts = [0]
+    for n in sizes:
+        cuts.append(cuts[-1] + n)
+    piece = [early_all[:, cuts[i] : cuts[i + 1]] for i in range(4)]
+
+    def half(x, w):
+        return lax.dynamic_index_in_dim(x.reshape(2 * shards, rank, 2, w), t, 2, keepdims=False)
+
+    grad_a_down = total(half(piece[0], ffw), 3).transpose(0, 2, 1)
+    grad_b_up = total(half(piece[1], ffw), 2)
+    grad_a_out = total(half(piece[2], width), 1).transpose(0, 2, 1)
+    rep_all = piece[3].reshape(2 * shards, 3, rank, features)
+    grad_b_out = total(rep_all[:, 0], 1)
+    grad_a_up = total(rep_all[:, 1], 2).transpose(0, 2, 1)
+    grad_b_down = total(rep_all[:, 2], 3)
+
+    late = jnp.concatenate([g_b_qkv, g_a_qkv], axis=1)
+    late_all = lax.all_gather(late, both, axis=0)
+    n = g_b_qkv.shape[1]
+    grad_b_qkv = total(
+        lax.dynamic_index_in_dim(
+            late_all[:, :, :n].reshape(2 * shards, rank, 2, n // 2), t, 2, keepdims=False
+        ),
+        0,
+    ).reshape(slots, rank, 3, width)
+    grad_a_qkv = total(late_all[:, :, n:], 0).transpose(0, 2, 1)
+    return (
+        out, grad_input, grad_a_qkv, grad_b_qkv, grad_a_out, grad_b_out,
+        grad_a_up, grad_b_up, grad_a_down, grad_b_down,
+    )
+
+
 def solution(mesh):
     placed = (
         P(("dp", "tensor"), None),
@@ -372,8 +1080,9 @@
         P("dp", None),
         P(("dp", "tensor"), None),
     )
+    paired = mesh.shape["tensor"] == 2 and mesh.shape["dp"] % 2 == 0
     return jax.shard_map(
-        per_device,
+        chip_device if paired else per_device,
         mesh=mesh,
         in_specs=placed,
         out_specs=(

time: 2580 us -> 716 us (0.28)
  matrix products: 1030 us -> 11.3 us
  waiting for transfers between devices: 1200 us -> 183 us
  Pallas kernels: 0 us -> 282 us
  other arithmetic: 123 us -> 19.2 us
  local copies, waits for them, and re-layouts: 148 us -> 94.9 us
  blocking collectives: 28.6 us -> 74.8 us
    dot_general x74 -> x8, matrix products: 960 us -> 11.3 us  [total(): lax.dot_general(onehot, mine_only, (((1,), (0,)), ((), ())), preferred_el...]
    reduce_scatter x11 -> x0, waiting for transfers between devices: 508 us -> none  [the longest x3 305 us: leave_rows(): lax.psum_scatter(partial_value, 'tensor', scatter_dimension=0, tiled=True)]
    all_gather x14 -> x4, waiting for transfers between devices: 463 us -> 144 us  [the longest x1 74.5 us: chip_device(): early_all = lax.all_gather(early_flat, both, axis=0).reshape(2 * shards, -1)]
    pallas_call x0 -> x5, Pallas kernels: none -> 282 us  [the longest x1 125 us: middle(): pl.pallas_call(functools.partial(middle_kernel, nf), out_shape=(jax.Shape...]
    psum x2 -> x0, waiting for transfers between devices: 225 us -> none  [the longest x1 137 us: per_device(): lax.psum((spread(grad_a_qkv_here, 0), spread(grad_b_out_here, 1), spread(...]
    dynamic_update_slice x24 -> x0, local copies, waits for them, and re-layouts: 93.4 us -> none  [the longest x8 85 us: attend_back(): lax.scan(one_block, (initial, initial), (numbers, log_sums))]
    sub x4 -> x0, matrix products: 72.9 us -> none  [one_block(): raised = jnp.exp(scores - peak)]
    reduce_sum x35 -> x0, other arithmetic: 71.2 us -> none  [the longest x4 60 us: one_block(): totals = jnp.sum(raised, axis=-1, keepdims=True)]
  transfers between devices with their start and end apart: 27 -> 10, of which waited for: 22 -> 5; matrix products, arithmetic and copies ran while one was open for 23% -> 7% of each run, Pallas kernels for 0% -> 9%
where the time goes in v1:
time: 716 us; the launch traced here: 709 us
  Pallas kernels  282 us (39%)
  waiting for transfers between devices  183 us (26%)
  local copies, waits for them, and re-layouts  94.9 us (13%)
  blocking collectives  74.8 us (10%)
  between operations  30.2 us (4%)
  other arithmetic  19.2 us (3%)
  starting transfers between devices  12.9 us (2%)
  matrix products  11.3 us (2%)
    pallas_call x1, Pallas kernels, middle(): pl.pallas_call(functools.partial(middle_kernel, nf), out_shape=(jax.Shape...  125 us
    all_gather x1, waiting for transfers between devices, chip_device(): early_all = lax.all_gather(early_flat, both, axis=0).reshape(2 * shards, -1)  74.5 us
    pallas_call x1, Pallas kernels, attend_rows_back(): pl.pallas_call(functools.partial(attend_back_kernel, bq, bk), out_shape=j...  71.9 us
    pallas_call x1, Pallas kernels, attend_rows(): pl.pallas_call(functools.partial(attend_kernel, bq), out_shape=(jax.Shape...  47.7 us
    all_to_all x4, blocking collectives, across(): return lax.all_to_all(x, 'dp', 0, 0, axis_index_groups=cores, tiled=True)  44 us
    all_gather x1, waiting for transfers between devices, chip_device(): rest_full = lax.all_gather(rest_shard, both, axis=0)  40.5 us
    ppermute x1, waiting for transfers between devices, chip_device(): far_half = lax.ppermute(shared_pick(theirs), 'tensor', [(0, 1), (1, 0)])  39.1 us
    all_gather x1, blocking collectives, chip_device(): all_marks = lax.all_gather(adapter_idx[0], 'dp', axis=0)  30.8 us
  transfers between devices with their start and end apart: 10, of which 5 were waited for; matrix products, arithmetic and copies ran while one was open for 7% of the time, Pallas kernels for 9%

profile of v1, /device:TPU:0, one launch (start us, length us, event | category | flops | bytes accessed | tf_op | source)
XLA Modules:
  0.0 709.2 jit_solution(18431118141568614945)
XLA Ops:
  35.5 4.1 collective-permute-start.1
  42.8 39.1 %collective-permute-done.1 = bf16[16,6144]{1,0:T(8,128)(2,1)S(1)} collective-permute-done((bf16[16,6144]{1,0:T(8,128)(2,1)S(1)}, bf16[16,6144]{1,0:T(8,128)(2,1)S(1)}, u32[]{:S(2)}, u32[]{:S(2)}) %collective-permute-start.1) | collective-permute-done | bytes 196640 | tf_op jit(solution)/shard_map/ppermute | solution.py:977
  86.1 4.1 all-gather.13.cloned.1.call-done
  90.2 14.8 %project_qkv.1 = (bf16[2,3,1024,512]{3,2,1,0:T(8,128)(2,1)}, bf16[1024,1024]{1,0:T(8,128)(2,1)S(1)}, bf16[1024,16]{1,0:T(8,128)(2,1)S(1)}) custom-call(bf16[1024,1024]{1,0:T(8,128)(2,1)S(1)} %broadcast_select_fusion.2.tok_ref, f32[1,1024]{1,0:T(1,128)S(1)} %bitcast.141, f32[1,1024]{1,0:T(1,128)S(1)} %bitcast.142, ...), custom_call_target="tpu_custom_call" | custom-call | tf_op jit(solution)/shard_map/project_qkv/pallas_call | solution.py:619
  107.1 15.2 %all_to_all.20.q_ref.k_ref.v_ref = bf16[2,3,1024,512]{3,2,1,0:T(8,128)(2,1)} all-to-all(bf16[2,3,1024,512]{3,2,1,0:T(8,128)(2,1)} %get-tuple-element.23), channel_id=1, replica_groups={{0,2},{4,6},{8,10},{12,14},{16,18},{20,22},{24,26},{28,30},{1,3},{5,7},..., dimensions={0} | all-to-all | bytes 12582912 | tf_op jit(solution)/shard_map/all_to_all | solution.py:949
  122.3 47.7 %attend.1 = (bf16[2,1024,512]{2,1,0:T(8,128)(2,1)S(1)}, f32[4,2,2048]{2,1,0:T(2,128)S(1)}) custom-call(s32[2]{0:T(128)S(1)} %slice.88.starts_ref, bf16[2,3,1024,512]{3,2,1,0:T(8,128)(2,1)} %all_to_all.20.q_ref.k_ref.v_ref, bf16[2,3,1024,512]{3,2,1,0:T(8,128)(2,1)} %all_to_all.20.q_ref.k_ref.v_ref, bf16[2,3,1024,512]{3,2,1,0:T(8,128)(2,1)} %all_to_all.20.q_ref.k_ref.v_ref), custom_call_target="tpu_custom_call" | custom-call | tf_op jit(solution)/shard_map/attend/pallas_call | solution.py:439
  170.0 6.5 all_to_all.21.mix_ref
  176.5 40.5 %all-gather.11.cloned.1.call-done = bf16[2048,4608]{1,0:T(8,128)(2,1)} async-done(((bf16[64,4608]{1,0:T(8,128)(2,1)}), bf16[2048,4608]{1,0:T(8,128)(2,1)}) %all-gather.11.cloned.1.call-update) | async-done | bytes 18874384 | tf_op jit(solution)/shard_map/all_gather | solution.py:988
  217.0 125.2 %middle.1 = (bf16[1024,1024]{1,0:T(8,128)(2,1)}, f32[1024,1024]{1,0:T(8,128)}, bf16[2,1024,512]{2,1,0:T(8,128)(2,1)}, bf16[10,32,512]{2,1,0:T(8,128)(2,1)}, bf16[3,16,1024]{2,1,0:T(8,128)(2,1)}) custom-call(s32[28]{0:T(128)} %constant.84.clone.tt_ref, s32[28]{0:T(128)} %constant.85.clone.cc_ref, s32[28]{0:T(128)} %constant.86.clone.sc_ref, ...), custom_call_target="tpu_custom_call" | custom-call | tf_op jit(solution)/shard_map/middle/pallas_call | solution.py:891
  342.2 7.0 all_to_all.22.do_ref
  349.2 71.9 %attend_back.1 = bf16[2,3,1024,512]{3,2,1,0:T(8,128)(2,1)} custom-call(s32[2]{0:T(128)S(1)} %slice.88.starts_ref, bf16[2,3,1024,512]{3,2,1,0:T(8,128)(2,1)} %all_to_all.20.q_ref.k_ref.v_ref, bf16[2,3,1024,512]{3,2,1,0:T(8,128)(2,1)} %all_to_all.20.q_ref.k_ref.v_ref, bf16[2,3,1024,512]{3,2,1,0:T(8,128)(2,1)} %all_to_all.20.q_ref.k_ref.v_ref, ...), custom_call_target="tpu_custom_call" | custom-call | tf_op jit(solution)/shard_map/attend_back/pallas_call | solution.py:546
  421.2 15.2 %all_to_all.23.g_ref = bf16[2,3,1024,512]{3,2,1,0:T(8,128)(2,1)} all-to-all(bf16[2,3,1024,512]{3,2,1,0:T(8,128)(2,1)} %attend_back.1), channel_id=1, replica_groups={{0,2},{4,6},{8,10},{12,14},{16,18},{20,22},{24,26},{28,30},{1,3},{5,7},..., dimensions={0} | all-to-all | bytes 12582912 | tf_op jit(solution)/shard_map/all_to_all | solution.py:949
  436.4 22.7 %project_qkv_back.1 = (f32[1024,1024]{1,0:T(8,128)}, bf16[16,3072]{1,0:T(8,128)(2,1)}, bf16[16,1024]{1,0:T(8,128)(2,1)}) custom-call(bf16[2,3,1024,512]{3,2,1,0:T(8,128)(2,1)} %all_to_all.23.g_ref, bf16[16,2,3,64,512]{4,3,2,1,0:T(8,128)(2,1)} %bitcast.147, bf16[2,16,6144]{2,1,0:T(8,128)(2,1)} %copy-done.3, bf16[16,1024]{1,0:T(8,128)(2,1)} %copy-done.5, ...), custom_call_target="tpu_custom_call" | custom-call | tf_op jit(solution)/shard_map/project_qkv_back/pallas_call | solution.py:685
  470.2 30.8 %all-gather.3 = s32[16,1,4]{2,1,0:T(1,128)S(1)} all-gather(s32[1,1,4]{2,1,0:T(1,128)S(1)} %bitcast.174), channel_id=1, replica_groups=mesh['dp'=16,'tensor'=2] {'dp'}, dimensions={0}, use_global_device_ids=true | all-gather | bytes 272 | tf_op jit(solution)/shard_map/all_gather | solution.py:990
  506.9 4.4 convert_select_fusion
  511.3 24.5 %all-gather.15.cloned.1.call-done = bf16[512,4096]{1,0:T(8,128)(2,1)} async-done(((bf16[16,4096]{1,0:T(8,128)(2,1)}), bf16[512,4096]{1,0:T(8,128)(2,1)}) %all-gather.15.cloned.1.call-update) | async-done | bytes 4194320 | tf_op jit(solution)/shard_map/all_gather | solution.py:1045
  545.2 5.7 constant_dynamic-slice_fusion.2
  552.4 4.6 reshape.149
  559.6 74.5 %all-gather.9.cloned.1.call-done = bf16[32,192,1024]{2,1,0:T(8,128)(2,1)} async-done(((bf16[1,192,1024]{2,1,0:T(8,128)(2,1)}), bf16[32,192,1024]{2,1,0:T(8,128)(2,1)}) %all-gather.9.cloned.1.call-update) | async-done | bytes 12582928 | tf_op jit(solution)/shard_map/all_gather | solution.py:1026
  634.1 11.9 %copy.132 = bf16[4,8,192,1024]{3,1,2,0:T(8,128)(2,1)S(1)} copy(bf16[4,8,192,1024]{3,2,1,0:T(8,128)(2,1)} %bitcast.149) | data formatting | bytes 25165824
  664.4 6.8 reshape.103
  671.2 7.0 constant_dynamic-slice_fusion
  682.1 6.9 reshape.104
  689.0 7.0 constant_dynamic-slice_fusion.3
  (119 shorter events, 80.7 us)
Async XLA Ops:
  7.2 32.5 %copy-start = (bf16[8,16,1024]{2,1,0:T(8,128)(2,1)S(1)}, bf16[8,16,1024]{2,1,0:T(8,128)(2,1)}, u32[]{:S(2)}) copy-start(bf16[8,16,1024]{2,1,0:T(8,128)(2,1)} %param.47) | copy-start | bytes 786436
  7.2 83.0 %all-gather.13.cloned.1.call-start = ((), (), s32[]{:S(2)}) async-start(), calls=%async_computation.6 | async-start | bytes 6488064 | tf_op jit(solution)/shard_map/all_gather | solution.py:986
  7.9 209.1 %all-gather.11.cloned.1.call-start = ((), (), s32[]{:S(2)}) async-start(), calls=%async_computation.5 | async-start | bytes 19464192 | tf_op jit(solution)/shard_map/all_gather | solution.py:988
  9.9 525.9 %all-gather.15.cloned.1.call-start = ((), (), s32[]{:S(2)}) async-start(), calls=%async_computation.7 | async-start | bytes 4325376 | tf_op jit(solution)/shard_map/all_gather | solution.py:1045
  10.7 4.5 collective-permute-start
  11.1 70.9 %collective-permute-start.2 = (bf16[1024,1024]{1,0:T(8,128)(2,1)}, bf16[1024,1024]{1,0:T(8,128)(2,1)}, u32[]{:S(2)}, u32[]{:S(2)}) collective-permute-start(bf16[1024,1024]{1,0:T(8,128)(2,1)} %param.31), channel_id=1, source_target_pairs={{2,1},{1,2},{6,5},{5,6},{10,9},{9,10},{14,13},{13,14},{18,17},{17,... | collective-permute-start | bytes 6291464 | tf_op jit(solution)/shard_map/ppermute | solution.py:946
  13.2 70.9 %collective-permute-start.3 = (bf16[1024,1024]{1,0:T(8,128)(2,1)}, bf16[1024,1024]{1,0:T(8,128)(2,1)}, u32[]{:S(2)}, u32[]{:S(2)}) collective-permute-start(bf16[1024,1024]{1,0:T(8,128)(2,1)} %param.50), channel_id=1, source_target_pairs={{2,1},{1,2},{6,5},{5,6},{10,9},{9,10},{14,13},{13,14},{18,17},{17,... | collective-permute-start | bytes 6291464 | tf_op jit(solution)/shard_map/ppermute | solution.py:946
  35.5 46.4 %collective-permute-start.1 = (bf16[16,6144]{1,0:T(8,128)(2,1)S(1)}, bf16[16,6144]{1,0:T(8,128)(2,1)S(1)}, u32[]{:S(2)}, u32[]{:S(2)}) collective-permute-start(bf16[16,6144]{1,0:T(8,128)(2,1)S(1)} %pad_maximum_fusion.4), channel_id=1, source_target_pairs={{0,1},{1,0},{2,3},{3,2},{4,5},{5,4},{6,7},{7,6},{8,9},{9,8},{10,11... | collective-permute-start | bytes 589832 | tf_op jit(solution)/shard_map/ppermute | solution.py:977
  42.6 47.6 %copy-start.5 = (bf16[16,1024]{1,0:T(8,128)(2,1)}, bf16[16,1024]{1,0:T(8,128)(2,1)S(1)}, u32[]{:S(2)}) copy-start(bf16[16,1024]{1,0:T(8,128)(2,1)S(1)} %dynamic-slice_bitcast_fusion.5.low_in_ref) | copy-start | bytes 98308
  82.0 8.2 %copy-start.3 = (bf16[2,16,6144]{2,1,0:T(8,128)(2,1)}, bf16[2,16,6144]{2,1,0:T(8,128)(2,1)S(1)}, u32[]{:S(2)}) copy-start(bf16[2,16,6144]{2,1,0:T(8,128)(2,1)S(1)} %pad_maximum_fusion.1.low_up_ref.sh_ref) | copy-start | bytes 1179652
  82.0 2.4 copy-start.10
  84.1 6.1 copy-start.2
  84.1 6.1 copy-start.7
  84.1 6.1 copy-start.8
  436.4 24.3 %copy-start.13 = (bf16[3,16,1024]{2,1,0:T(8,128)(2,1)S(1)}, bf16[3,16,1024]{2,1,0:T(8,128)(2,1)}, u32[]{:S(2)}) copy-start(bf16[3,16,1024]{2,1,0:T(8,128)(2,1)} %get-tuple-element.35) | copy-start | bytes 294916
  436.4 24.4 %copy-start.12 = (bf16[10,32,512]{2,1,0:T(8,128)(2,1)S(1)}, bf16[10,32,512]{2,1,0:T(8,128)(2,1)}, u32[]{:S(2)}) copy-start(bf16[10,32,512]{2,1,0:T(8,128)(2,1)} %get-tuple-element.34) | copy-start | bytes 983044
  460.7 1.6 copy-start.11
  460.7 173.4 %all-gather.9.cloned.1.call-start = ((), (), s32[]{:S(2)}) async-start(), calls=%async_computation.4 | async-start | bytes 12976128 | tf_op jit(solution)/shard_map/all_gather | solution.py:1026
  462.3 41.7 %collective-permute-start.4 = (bf16[1024,1024]{1,0:T(8,128)(2,1)S(1)}, bf16[1024,1024]{1,0:T(8,128)(2,1)}, u32[]{:S(2)}, u32[]{:S(2)}) collective-permute-start(bf16[1024,1024]{1,0:T(8,128)(2,1)S(1)} %copy-done.11), channel_id=1, source_target_pairs={{2,1},{1,2},{6,5},{5,6},{10,9},{9,10},{14,13},{13,14},{18,17},{17,... | collective-permute-start | bytes 6291464 | tf_op jit(solution)/shard_map/ppermute | solution.py:946
  464.3 5.9 copy-start.14
  464.3 36.8 %copy-start.15 = (s32[32]{0:T(128)S(1)}, s32[32]{0:T(128)}, u32[]{:S(2)}) copy-start(s32[32]{0:T(128)} %constant.94) | copy-start | bytes 388
  468.2 37.3 %collective-permute-start.5 = (bf16[1024,1024]{1,0:T(8,128)(2,1)}, bf16[1024,1024]{1,0:T(8,128)(2,1)}, u32[]{:S(2)}, u32[]{:S(2)}) collective-permute-start(bf16[1024,1024]{1,0:T(8,128)(2,1)} %convert_element_type.4), channel_id=1, source_target_pairs={{2,1},{1,2},{6,5},{5,6},{10,9},{9,10},{14,13},{13,14},{18,17},{17,... | collective-permute-start | bytes 6291464 | tf_op jit(solution)/shard_map/ppermute | solution.py:946
  504.0 3.0 copy-start.9
  696.0 6.2 copy-start.1
  (2 other events, 2.0 us)
Sparse Core Ops, SparseCore 0:
  10.9 79.2 all-gather.12
  93.7 123.3 all-gather.10
  460.8 74.8 all-gather.14
  539.1 95.0 all-gather.8
